TPU v7x, 256 devices: a whole 4x4x8 slice. The times are simulated.
256 devices in a mesh: section: 4 (over x), shard: 64 (over z, y, core).
Axes of the slice: x: 4, y: 4, z: 8, core: 2. Of those that a mesh axis runs over, the one named last changes fastest.
Arguments:
- features: bfloat16 [4096, 768], P('shard'), may hold values from -6 to 6
- tile_cols: int32 [4, 32, 16], P('section'), may hold values from 0 to 31
- live_tiles: int32 [4, 32], P('section'), may hold values from 1 to 16, 256 in all within a row
- tile_values: bfloat16 [4, 4096, 16, 128], P('section', 'shard'), may hold values from -0.375 to 0.375
- degrees: int32 [4, 4096], P('section', 'shard'), may hold values from 1 to 8
Outputs:
- hops: bfloat16 [4, 4096, 768], P('section', 'shard')
Inputs may be any that keep to these rules, and one draw needn't show every extreme that they name: `live_tiles`: every row block has at least one live tile slot; the live counts of one relation sum to 256.
All inputs are finite; a program needn't handle non-finite values.
Results may differ from a plain program's by a relative error of at most 0.0056.
Values may be sent and summed in bfloat16 or wider, within the bound.
A program may use at most 64 MiB of HBM per device.

v0:
```python
import jax
import jax.numpy as jnp
from jax import lax
from jax.sharding import PartitionSpec as P


def from_behind(value, axis, by):
    peers = lax.axis_size(axis)
    pairs = [(i, i + by) for i in range(peers) if 0 <= i + by < peers]
    return lax.ppermute(value, axis, pairs)


def propagate(gathered, block_ids, live_count, tile_rows, row_scale):
    tile_size = tile_rows.shape[2]
    width = gathered.shape[1]
    blocks = gathered.reshape(gathered.shape[0] // tile_size, tile_size, width)
    source = blocks[block_ids]
    live_mask = (jnp.arange(tile_rows.shape[1], dtype=jnp.int32) < live_count).astype(jnp.bfloat16)
    masked = tile_rows * live_mask[None, :, None]
    summed = jnp.einsum("rkc,kcw->rw", masked, source, preferred_element_type=jnp.float32)
    return (summed * row_scale[:, None]).astype(jnp.bfloat16)


def per_device(features, tile_cols, live_tiles, tile_values, degrees):
    section_index = lax.axis_index("section")
    section_count = lax.axis_size("section")
    tile_rows = tile_values[0]
    row_count = tile_rows.shape[0]
    tile_size = tile_rows.shape[2]
    block_row = lax.axis_index("shard") * row_count // tile_size
    block_ids = lax.dynamic_index_in_dim(tile_cols[0], block_row, 0, keepdims=False)
    live_count = lax.dynamic_index_in_dim(live_tiles[0], block_row, 0, keepdims=False)
    row_scale = lax.rsqrt(degrees[0].astype(jnp.float32))
    width = features.shape[1]
    result = jnp.zeros((row_count, width), jnp.bfloat16)
    arrived = jnp.zeros((row_count, width), jnp.bfloat16)
    for hop_num in range(section_count):
        slab_in = jnp.where(section_index == 0, features, arrived)
        gathered = lax.all_gather(slab_in, "shard", axis=0, tiled=True)
        output = propagate(gathered, block_ids, live_count, tile_rows, row_scale)
        result = jnp.where(section_index == hop_num, output, result)
        arrived = from_behind(output, "section", 1)
    return result[None]


def solution(mesh):
    in_specs = (
        P("shard", None),
        P("section", None, None),
        P("section", None),
        P("section", "shard", None, None),
        P("section", "shard"),
    )
    out_specs = P("section", "shard", None)
    return jax.shard_map(
        per_device, mesh=mesh, in_specs=in_specs, out_specs=out_specs, check_vma=False
    )
```

profile of v0, /device:TPU:7, one launch (start us, length us, event | category | flops | bytes accessed | tf_op | source)
XLA Modules:
  0.0 374.5 jit_solution(7608889095608387722)
XLA Ops:
  6.5 0.0 copy-start
  6.5 0.0 all-gather.5.cloned.1.call-start
  6.5 0.7 broadcast_select_fusion.3
  7.2 0.1 all-gather.5.cloned.1.call-update
  7.3 0.0 all-gather.7.cloned.1.call-start
  7.3 1.3 constant_dynamic-slice_fusion
  8.6 0.0 copy-done
  8.6 0.2 dynamic-slice_reduce_fusion
  8.8 0.6 compare_convert_fusion
  9.5 0.7 rsqrt_bitcast_fusion
  10.1 1.0 bitcast_multiply_fusion
  11.2 82.8 %all-gather.5.cloned.1.call-done = bf16[4096,768]{1,0:T(8,128)(2,1)} async-done(((bf16[64,768]{1,0:T(8,128)(2,1)}), bf16[4096,768]{1,0:T(8,128)(2,1)}) %all-gather.5.cloned.1.call-update) | async-done | bytes 6291472 | tf_op jit(solution)/shard_map/all_gather | solution.py:39
  94.0 3.5 gather_fusion
  97.5 0.0 copy-start.1
  97.5 0.7 fusion.4
  98.2 0.0 copy-start.2
  98.2 0.6 copy-done.2
  98.9 1.3 collective-permute-start
  100.1 4.7 %collective-permute-done = bf16[64,768]{1,0:T(8,128)(2,1)S(1)} collective-permute-done((bf16[64,768]{1,0:T(8,128)(2,1)S(1)}, bf16[64,768]{1,0:T(8,128)(2,1)S(1)}, u32[]{:S(2)}, u32[]{:S(2)}) %collective-permute-start) | collective-permute-done | bytes 98336 | tf_op jit(solution)/shard_map/ppermute | solution.py:10
  104.8 0.0 copy-done.1
  104.8 0.7 broadcast_select_fusion.2
  105.5 0.0 all-gather.7.cloned.1.call-update
  105.5 0.0 all-gather.9.cloned.1.call-start
  105.5 78.2 %all-gather.7.cloned.1.call-done = bf16[4096,768]{1,0:T(8,128)(2,1)} async-done(((bf16[64,768]{1,0:T(8,128)(2,1)}), bf16[4096,768]{1,0:T(8,128)(2,1)}) %all-gather.7.cloned.1.call-update) | async-done | bytes 6291472 | tf_op jit(solution)/shard_map/all_gather | solution.py:39
  183.7 3.5 gather_fusion.1
  187.2 0.7 fusion.5
  187.9 0.0 copy-start.4
  187.9 0.6 copy-done.4
  188.6 1.3 collective-permute-start.1
  189.8 4.7 %collective-permute-done.1 = bf16[64,768]{1,0:T(8,128)(2,1)S(1)} collective-permute-done((bf16[64,768]{1,0:T(8,128)(2,1)S(1)}, bf16[64,768]{1,0:T(8,128)(2,1)S(1)}, u32[]{:S(2)}, u32[]{:S(2)}) %collective-permute-start.1) | collective-permute-done | bytes 98336 | tf_op jit(solution)/shard_map/ppermute | solution.py:10
  194.5 0.7 broadcast_select_fusion.1
  195.2 0.0 all-gather.9.cloned.1.call-update
  195.2 0.0 all-gather.11.cloned.1.call-start
  195.3 78.2 %all-gather.9.cloned.1.call-done = bf16[4096,768]{1,0:T(8,128)(2,1)} async-done(((bf16[64,768]{1,0:T(8,128)(2,1)}), bf16[4096,768]{1,0:T(8,128)(2,1)}) %all-gather.9.cloned.1.call-update) | async-done | bytes 6291472 | tf_op jit(solution)/shard_map/all_gather | solution.py:39
  273.4 3.5 gather_fusion.2
  276.9 0.7 fusion.6
  277.6 0.0 copy-start.5
  277.6 0.6 copy-done.5
  278.3 1.3 collective-permute-start.2
  279.5 4.7 %collective-permute-done.2 = bf16[64,768]{1,0:T(8,128)(2,1)S(1)} collective-permute-done((bf16[64,768]{1,0:T(8,128)(2,1)S(1)}, bf16[64,768]{1,0:T(8,128)(2,1)S(1)}, u32[]{:S(2)}, u32[]{:S(2)}) %collective-permute-start.2) | collective-permute-done | bytes 98336 | tf_op jit(solution)/shard_map/ppermute | solution.py:10
  284.2 0.7 broadcast_select_fusion
  284.9 0.0 all-gather.11.cloned.1.call-update
  284.9 78.2 %all-gather.11.cloned.1.call-done = bf16[4096,768]{1,0:T(8,128)(2,1)} async-done(((bf16[64,768]{1,0:T(8,128)(2,1)}), bf16[4096,768]{1,0:T(8,128)(2,1)}) %all-gather.11.cloned.1.call-update) | async-done | bytes 6291472 | tf_op jit(solution)/shard_map/all_gather | solution.py:39
  363.1 0.0 copy-start.3
  363.1 3.6 gather_fusion.3
  366.7 0.0 copy-done.3
  366.7 1.3 fusion.9
  (2 shorter events, 0.0 us)
Async XLA Ops:
  6.5 2.1 copy-start
  6.5 87.5 %all-gather.5.cloned.1.call-start = ((), (), s32[]{:S(2)}) async-start(), calls=%async_computation | async-start | bytes 6389760 | tf_op jit(solution)/shard_map/all_gather | solution.py:39
  7.3 176.4 %all-gather.7.cloned.1.call-start = ((), (), s32[]{:S(2)}) async-start(), calls=%async_computation.1 | async-start | bytes 6389760 | tf_op jit(solution)/shard_map/all_gather | solution.py:39
  97.5 7.3 %copy-start.1 = (bf16[64,768]{1,0:T(8,128)(2,1)S(1)}, bf16[64,768]{1,0:T(8,128)(2,1)}, u32[]{:S(2)}) copy-start(bf16[64,768]{1,0:T(8,128)(2,1)} %param.5) | copy-start | bytes 294916
  98.2 0.6 copy-start.2
  98.9 6.0 %collective-permute-start = (bf16[64,768]{1,0:T(8,128)(2,1)S(1)}, bf16[64,768]{1,0:T(8,128)(2,1)S(1)}, u32[]{:S(2)}, u32[]{:S(2)}) collective-permute-start(bf16[64,768]{1,0:T(8,128)(2,1)S(1)} %fusion.4), channel_id=1, source_target_pairs={{0,64},{64,128},{128,192},{1,65},{65,129},{129,193},{2,66},{66,130... | collective-permute-start | bytes 294920 | tf_op jit(solution)/shard_map/ppermute | solution.py:10
  105.5 167.9 %all-gather.9.cloned.1.call-start = ((), (), s32[]{:S(2)}) async-start(), calls=%async_computation.2 | async-start | bytes 6389760 | tf_op jit(solution)/shard_map/all_gather | solution.py:39
  187.9 0.6 copy-start.4
  188.6 6.0 %collective-permute-start.1 = (bf16[64,768]{1,0:T(8,128)(2,1)S(1)}, bf16[64,768]{1,0:T(8,128)(2,1)S(1)}, u32[]{:S(2)}, u32[]{:S(2)}) collective-permute-start(bf16[64,768]{1,0:T(8,128)(2,1)S(1)} %fusion.5), channel_id=1, source_target_pairs={{0,64},{64,128},{128,192},{1,65},{65,129},{129,193},{2,66},{66,130... | collective-permute-start | bytes 294920 | tf_op jit(solution)/shard_map/ppermute | solution.py:10
  195.2 167.9 %all-gather.11.cloned.1.call-start = ((), (), s32[]{:S(2)}) async-start(), calls=%async_computation.3 | async-start | bytes 6389760 | tf_op jit(solution)/shard_map/all_gather | solution.py:39
  277.6 0.6 copy-start.5
  278.3 6.0 %collective-permute-start.2 = (bf16[64,768]{1,0:T(8,128)(2,1)S(1)}, bf16[64,768]{1,0:T(8,128)(2,1)S(1)}, u32[]{:S(2)}, u32[]{:S(2)}) collective-permute-start(bf16[64,768]{1,0:T(8,128)(2,1)S(1)} %fusion.6), channel_id=1, source_target_pairs={{0,64},{64,128},{128,192},{1,65},{65,129},{129,193},{2,66},{66,130... | collective-permute-start | bytes 294920 | tf_op jit(solution)/shard_map/ppermute | solution.py:10
  363.1 3.6 copy-start.3
Sparse Core Ops, SparseCore 0:
  10.1 83.8 all-gather.4
  105.6 78.0 all-gather.6
  195.3 78.0 all-gather.8
  285.0 78.0 all-gather.10
where the time goes:
time: 376 us; the launch traced here: 375 us
  waiting for transfers between devices  331 us (88%)
  local copies, waits for them, and re-layouts  17.5 us (5%)
  between operations  13.3 us (4%)
  other arithmetic  4.97 us (1%)
  starting transfers between devices  3.97 us (1%)
    all_gather x4, waiting for transfers between devices, per_device(): gathered = lax.all_gather(slab_in, 'shard', axis=0, tiled=True)  317 us
    gather x4, local copies, waits for them, and re-layouts, propagate(): source = blocks[block_ids]  14.2 us
    ppermute x3, waiting for transfers between devices, from_behind(): return lax.ppermute(value, axis, pairs)  14 us
  transfers between devices with their start and end apart: 7, of which 7 were waited for; matrix products, arithmetic and copies ran while one was open for 1% of the time, Pallas kernels for 0%

commit v1 on v0

v1 whole, which is shorter than its diff:
```python
import jax
import jax.numpy as jnp
from jax import lax
from jax.experimental import pallas as pl
from jax.experimental.pallas import tpu as pltpu
from jax.sharding import PartitionSpec as P

MESH = pl.DeviceIdType.MESH
X, Y, Z = 4, 4, 8
HOPS = 4
TILE = 128
SLOTS = 16
COLS = 96
BLOCKS = Y * Z
HALF = 64
CHUNK = 16
SEND_UP = (0, 1, 2, 3)


def kernel(ft, a_in, meta, out, xg0, xg1, xg2, xg3, a_all, lhs, ybuf, half_x, mbuf, obuf, tbuf, sm,
           r_sem, s_sem, a_sem, c_sem, as_sem, m_sem, ms_sem, o_sem, os_sem, h_sem, l_sem):
    x = lax.axis_index("section")
    sh = lax.axis_index("shard")
    z, y, c = sh // 8, (sh // 2) % 4, sh % 2
    g = 2 * x + c
    xgs = (xg0, xg1, xg2, xg3)

    def at(dx=0, dy=0, dz=0, core=None):
        core = c if core is None else core
        return ((x + dx) % X, ((z + dz) % Z) * 8 + ((y + dy) % Y) * 2 + core)

    def blk(dy=0, dz=0):
        return ((y + dy) % Y) * Z + (z + dz) % Z

    def rows(core, first=0, count=HALF):
        return pl.ds(pl.multiple_of(core * HALF + first, 16), count)

    def send(src, dst, ssem, rsem, to):
        pltpu.make_async_remote_copy(src_ref=src, dst_ref=dst, send_sem=ssem, recv_sem=rsem,
                                     device_id=to, device_id_type=MESH).start()

    def arrived(ref, sem):
        pltpu.make_async_copy(ref, ref, sem).wait()

    other = 1 - c
    line = [(dx, same) for dx in range(X) for same in (True, False) if (dx, same) != (0, True)]

    barrier = pltpu.get_barrier_semaphore()
    peers = [at(dz=d) for d in range(1, Z)] + [at(dy=1), at(dy=-1)]
    peers += [at(dx=dx, core=c if same else other) for dx, same in line]
    for to in peers:
        pl.semaphore_signal(barrier, inc=1, device_id=to, device_id_type=MESH)
    pl.semaphore_wait(barrier, len(peers))

    sib = at(core=other)
    send(ft.at[other], half_x, h_sem.at[0], h_sem.at[1], sib)

    for q in range(4):
        for dx, k in ((1, q), (-1, 3 - q)):
            send(a_in.at[pl.ds(k * CHUNK, CHUNK)], a_all.at[x, rows(c, k * CHUNK, CHUNK)],
                 as_sem.at[0], a_sem.at[x, k], at(dx=dx))
    send(a_in, a_all.at[x, rows(c)], as_sem.at[2], c_sem.at[x], sib)
    own_a = pltpu.make_async_copy(a_in, a_all.at[x, rows(c)], l_sem.at[0])
    own_a.start()
    for dx, same in line:
        send(meta, mbuf.at[g], ms_sem.at[0], m_sem.at[g], at(dx=dx, core=c if same else other))
    mbuf[g] = meta[...]

    arrived(half_x, h_sem.at[1])
    xg0[blk()] = (ft[c].astype(jnp.float32) + half_x[...].astype(jnp.float32)).astype(jnp.bfloat16)

    def relay(h, dz):
        xg = xgs[h]
        if dz in SEND_UP:
            b, to = blk(-1, dz), at(dy=1)
        else:
            b, to = blk(1, dz), at(dy=-1)
        arrived(xg.at[b], r_sem.at[h, b])
        send(xg.at[b], xg.at[b], s_sem.at[h], r_sem.at[h, b], to)

    def spread(h, dz):
        xg = xgs[h]
        b = blk(0, dz)
        arrived(xg.at[b], r_sem.at[h, b])
        for dy in (1, -1):
            send(xg.at[b], xg.at[b], s_sem.at[h], r_sem.at[h, b], at(dy=dy))

    def gather_start(h, src):
        b = blk()
        for dz in (4, 3, -3, 2, -2, 1, -1):
            send(src, xgs[h].at[b], s_sem.at[h], r_sem.at[h, b], at(dz=dz))
        for dy in (1, -1):
            send(src, xgs[h].at[b], s_sem.at[h], r_sem.at[h, b], at(dy=dy))

    def gather_rest(h):
        relay(h, 0)
        spread(h, 1)
        spread(h, -1)
        spread(h, 2)
        spread(h, -2)
        relay(h, 1)
        relay(h, -1)
        spread(h, 3)
        spread(h, -3)
        relay(h, 2)
        relay(h, -2)
        spread(h, 4)
        relay(h, 3)
        relay(h, -3)
        relay(h, 4)
        for dz in (0, 1, -1, 2, -2, 3, -3, 4):
            b = blk(1 if dz in SEND_UP else -1, dz)
            arrived(xgs[h].at[b], r_sem.at[h, b])
        for dz in (0, 1, -1, 2, -2, 3, -3, 4):
            b = blk(2, dz)
            arrived(xgs[h].at[b], r_sem.at[h, b])

    def tile_chunk(s, k):
        ref = a_all.at[s, rows(c, k * CHUNK, CHUNK)]
        arrived(ref, a_sem.at[s, k])
        return ref

    def compute(h):
        for k in range(SLOTS):
            lhs[:, k * TILE:(k + 1) * TILE] = xgs[h][sm[2 * h, 1, k]]
        acc = lax.dot_general(lhs[...], a_all[h], (((1,), (1,)), ((), ())),
                              preferred_element_type=jnp.float32)
        degree = mbuf[2 * h, 0:1, :] + mbuf[2 * h + 1, 0:1, :]
        val = (acc * lax.rsqrt(degree.astype(jnp.float32))).astype(jnp.bfloat16)
        ybuf[h] = val
        if h < HOPS - 1:
            xgs[h + 1][blk()] = val
            gather_start(h + 1, ybuf.at[h])

        @pl.when(x == h)
        def _():
            obuf[g] = ybuf[h]
            send(ybuf.at[h], obuf.at[g], os_sem.at[0], o_sem.at[g], sib)

        @pl.when(x != h)
        def _():
            for core in (0, 1):
                send(ybuf.at[h], obuf.at[g], os_sem.at[0], o_sem.at[g], (h, (sh // 2) * 2 + core))

    gather_start(0, xg0.at[blk()])

    left, right, far = (x - 1) % X, (x + 1) % X, (x + 2) % X
    for q in range(2):
        for s, k, dx in ((left, q, 1), (right, 3 - q, -1)):
            ref = tile_chunk(s, k)
            send(ref, ref, as_sem.at[1], a_sem.at[s, k], at(dx=dx))
    gather_rest(0)
    for dx, same in line:
        p = 2 * ((x + dx) % X) + (c if same else other)
        arrived(mbuf.at[p], m_sem.at[p])
    to_sm = pltpu.make_async_copy(mbuf, sm, l_sem.at[1])
    to_sm.start()
    for s, ks in ((left, (2, 3)), (right, (1, 0)), (far, (0, 1, 2, 3))):
        for k in ks:
            tile_chunk(s, k)
        piece = a_all.at[s, rows(c)]
        send(piece, piece, as_sem.at[2], c_sem.at[s], sib)
    own_a.wait()
    for s in range(X):
        arrived(a_all.at[s, rows(other)], c_sem.at[s])
    to_sm.wait()
    compute(0)
    for h in range(1, HOPS):
        gather_rest(h)
        compute(h)

    for dx, same in line:
        p = 2 * ((x + dx) % X) + (c if same else other)
        arrived(obuf.at[p], o_sem.at[p])
    for i in range(8):
        tbuf[:, i * COLS:(i + 1) * COLS] = obuf[i].astype(jnp.float32).T
    out[...] = tbuf[pl.ds(pl.multiple_of(c * HALF, HALF), HALF), :].astype(jnp.bfloat16)

    arrived(half_x, h_sem.at[0])
    arrived(a_all.at[0], as_sem.at[0])
    arrived(a_all.at[0, pl.ds(0, HALF)], as_sem.at[1])
    arrived(a_all.at[pl.ds(0, 2)], as_sem.at[2])
    arrived(mbuf.at[pl.ds(0, 7)], ms_sem.at[0])
    arrived(obuf.at[pl.ds(0, 7)], os_sem.at[0])
    for h in range(HOPS):
        arrived(xgs[h].at[pl.ds(0, 31)], s_sem.at[h])


def per_device(features, tile_cols, live_tiles, tile_values, degrees):
    x = lax.axis_index("section")
    sh = lax.axis_index("shard")
    c = sh % 2
    row = sh // 2
    part = lax.dynamic_slice(features, (0, 2 * COLS * x), (HALF, 2 * COLS)).T
    zero = jnp.zeros_like(part)
    part = jnp.where(c == 0, jnp.concatenate([part, zero], 1), jnp.concatenate([zero, part], 1))
    ft = part.reshape(2, COLS, TILE)
    live = lax.dynamic_index_in_dim(live_tiles[0], row, 0, keepdims=False)
    mask = jnp.arange(SLOTS, dtype=jnp.int32) < live
    a_in = jnp.where(mask[None, :, None], tile_values[0], 0).reshape(HALF, SLOTS * TILE)
    cols = lax.dynamic_index_in_dim(tile_cols[0], row, 0, keepdims=False)
    cols = (cols % Y) * Z + cols // Y
    d = degrees[0]
    dz = jnp.zeros_like(d)
    d = jnp.where(c == 0, jnp.concatenate([d, dz]), jnp.concatenate([dz, d]))
    meta = jnp.concatenate([d[None], jnp.pad(cols, (0, TILE - SLOTS))[None],
                            jnp.zeros((6, TILE), jnp.int32)], 0)
    vm = pl.BlockSpec(memory_space=pltpu.VMEM)
    dma = pltpu.SemaphoreType.DMA
    slab = pltpu.VMEM((BLOCKS, COLS, TILE), jnp.bfloat16)
    res = pl.pallas_call(
        kernel,
        out_shape=jax.ShapeDtypeStruct((HALF, 8 * COLS), jnp.bfloat16),
        in_specs=[vm] * 3,
        out_specs=vm,
        scratch_shapes=[
            slab, slab, slab, slab,
            pltpu.VMEM((X, TILE, SLOTS * TILE), jnp.bfloat16),
            pltpu.VMEM((COLS, SLOTS * TILE), jnp.bfloat16),
            pltpu.VMEM((HOPS, COLS, TILE), jnp.bfloat16),
            pltpu.VMEM((COLS, TILE), jnp.bfloat16),
            pltpu.VMEM((8, 8, TILE), jnp.int32),
            pltpu.VMEM((8, COLS, TILE), jnp.bfloat16),
            pltpu.VMEM((TILE, 8 * COLS), jnp.float32),
            pltpu.SMEM((8, 8, TILE), jnp.int32),
            dma((HOPS, BLOCKS)), dma((HOPS,)), dma((X, 4)), dma((X,)), dma((3,)),
            dma((8,)), dma((1,)), dma((8,)), dma((1,)), dma((2,)), dma((2,)),
        ],
        compiler_params=pltpu.CompilerParams(collective_id=0, has_side_effects=True,
                                             vmem_limit_bytes=40 * 1024 * 1024),
        name="propagate",
    )(ft, a_in, meta)
    return res[None]


def solution(mesh):
    in_specs = (
        P("shard", None),
        P("section", None, None),
        P("section", None),
        P("section", "shard", None, None),
        P("section", "shard"),
    )
    return jax.shard_map(per_device, mesh=mesh, in_specs=in_specs,
                         out_specs=P("section", "shard", None), check_vma=False)
```

time: 376 us -> 88.6 us (0.24)
  waiting for transfers between devices: 331 us -> 0 us
  Pallas kernels: 0 us -> 83.6 us
  local copies, waits for them, and re-layouts: 17.5 us -> 3.16 us
  between operations: 13.3 us -> 0.06 us
  starting transfers between devices: 3.97 us -> 0 us
    all_gather x4 -> x0, waiting for transfers between devices: 317 us -> none  [per_device(): gathered = lax.all_gather(slab_in, 'shard', axis=0, tiled=True)]
    pallas_call x0 -> x1, Pallas kernels: none -> 83.6 us  [per_device(): pl.pallas_call(kernel, out_shape=jax.ShapeDtypeStruct((HALF, 8 * COLS), j...]
    gather x4 -> x0, local copies, waits for them, and re-layouts: 14.2 us -> none  [propagate(): source = blocks[block_ids]]
    ppermute x3 -> x0, waiting for transfers between devices: 14 us -> none  [from_behind(): return lax.ppermute(value, axis, pairs)]
    ppermute x3 -> x0, starting transfers between devices: 3.84 us -> none  [from_behind(): return lax.ppermute(value, axis, pairs)]
  transfers between devices with their start and end apart: 7 -> 0, of which waited for: 7 -> 0; matrix products, arithmetic and copies ran while one was open for 1% -> 0% of each run, Pallas kernels for 0% -> 0%
where the time goes in v1:
time: 88.6 us; the launch traced here: 88.4 us
  Pallas kernels  83.6 us (94%)
  local copies, waits for them, and re-layouts  3.16 us (4%)
  other arithmetic  1.62 us (2%)
    pallas_call x1, Pallas kernels, per_device(): pl.pallas_call(kernel, out_shape=jax.ShapeDtypeStruct((HALF, 8 * COLS), j...  83.6 us

profile of v1, /device:TPU:7, one launch (start us, length us, event | category | flops | bytes accessed | tf_op | source)
XLA Modules:
  0.0 88.4 jit_solution(995017207837676294)
XLA Ops:
  0.0 0.0 copy-start
  0.0 0.0 copy-start.1
  0.0 1.3 %constant_dynamic-slice_fusion = s32[1,1]{1,0:T(1,128)} fusion(s32[1,32]{1,0:T(1,128)} %param.7, s32[]{:T(128)S(6)} %select_n.57), kind=kLoop, calls=%fused_computation.12 | loop fusion | bytes 12 | tf_op jit(solution)/shard_map/jit(dynamic_index_in_dim)/dynamic_slice | solution.py:198
  1.3 0.6 iota_compare_fusion
  1.9 0.9 dynamic-slice_reduce_fusion
  2.9 0.1 pad.11.clone
  2.9 0.8 fusion
  3.7 0.1 broadcast_bitcast_fusion
  3.8 0.1 add_add_fusion.meta
  3.9 0.0 copy-done
  3.9 0.1 dynamic-slice_bitcast_fusion
  4.0 0.1 copy.7
  4.1 0.0 copy-done.1
  4.1 0.1 bitcast_select_fusion.a_in
  4.2 83.6 %propagate.1 = bf16[64,768]{1,0:T(8,128)(2,1)S(1)} custom-call(bf16[2,96,128]{2,1,0:T(8,128)(2,1)S(1)} %bitcast.17, bf16[64,2048]{1,0:T(8,128)(2,1)S(1)} %bitcast_select_fusion.a_in, s32[8,128]{1,0:T(8,128)S(1)} %add_add_fusion.meta), custom_call_target="tpu_custom_call" | custom-call | tf_op jit(solution)/shard_map/propagate/pallas_call | solution.py:211
  87.8 0.6 copy.11
  (3 shorter events, 0.0 us)
Async XLA Ops:
  0.0 3.9 %copy-start = (bf16[64,768]{1,0:T(8,128)(2,1)S(1)}, bf16[64,768]{1,0:T(8,128)(2,1)}, u32[]{:S(2)}) copy-start(bf16[64,768]{1,0:T(8,128)(2,1)} %param.5) | copy-start | bytes 294916
  0.0 4.1 %copy-start.1 = (bf16[1,64,16,128]{3,2,1,0:T(8,128)(2,1)S(1)}, bf16[1,64,16,128]{3,2,1,0:T(8,128)(2,1)}, u32[]{:S(2)}) copy-start(bf16[1,64,16,128]{3,2,1,0:T(8,128)(2,1)} %param.8) | copy-start | bytes 786436

commit v2 on v1

v2 whole, which is shorter than its diff:
```python
import jax
import jax.numpy as jnp
from jax import lax
from jax.experimental import pallas as pl
from jax.experimental.pallas import tpu as pltpu
from jax.sharding import PartitionSpec as P

MESH = pl.DeviceIdType.MESH
X, Y, Z = 4, 4, 8
HOPS = 4
TILE = 128
SLOTS = 16
COLS = 96
BLOCKS = Y * Z
HALF = 64
CHUNK = 16
DYS = (0, 1, -1, 2)
DZS = (0, 1, -1, 2, -2, 3, -3, 4)
COLS_AT = 8


def parent(dy, dz):
    if dy == 0 or dz == 0:
        return (0, 0)
    if abs(dz) == 1 or (abs(dz) == 2 and dy != 2):
        return (dy, 0)
    return (0, dz)


def far(o):
    return abs(o[0]) + abs(o[1])


OFFSETS = [(dy, dz) for dz in DZS for dy in DYS if dy or dz]
KIDS = {}
for _o in sorted(OFFSETS, key=lambda o: -far(o)):
    KIDS.setdefault(parent(*_o), []).append(_o)
DIRECT = sorted(KIDS.pop((0, 0)), key=lambda o: (o not in KIDS, -far(o)))
RELAYS = sorted(KIDS, key=far)
LEAVES = [o for o in sorted(OFFSETS, key=lambda o: (far(o) + far(parent(*o)), far(o))) if o not in KIDS]


def kernel(feat, cols, live, deg, a_in, out, xg0, xg1, xg2, xg3, a_all, lhs, ybuf, half_x, fpad, ft, meta, mbuf, obuf, sm,
           r_sem, s_sem, a_sem, c_sem, as_sem, m_sem, ms_sem, o_sem, os_sem, h_sem, l_sem):
    x = lax.axis_index("section")
    sh = lax.axis_index("shard")
    z, y, c = sh // 8, (sh // 2) % 4, sh % 2
    g = 2 * x + c
    xgs = (xg0, xg1, xg2, xg3)

    def at(dx=0, dy=0, dz=0, core=None):
        core = c if core is None else core
        return ((x + dx) % X, ((z + dz) % Z) * 8 + ((y + dy) % Y) * 2 + core)

    def blk(dy=0, dz=0):
        return ((y + dy) % Y) * Z + (z + dz) % Z

    def rows(core, first=0, count=HALF):
        return pl.ds(pl.multiple_of(core * HALF + first, 16), count)

    def cols_of(group):
        return pl.ds(pl.multiple_of(group * COLS, 16), COLS)

    def send(src, dst, ssem, rsem, to):
        pltpu.make_async_remote_copy(src_ref=src, dst_ref=dst, send_sem=ssem, recv_sem=rsem,
                                     device_id=to, device_id_type=MESH).start()

    def arrived(ref, sem):
        pltpu.make_async_copy(ref, ref, sem).wait()

    other = 1 - c
    line = [(dx, same) for dx in range(X) for same in (True, False) if (dx, same) != (0, True)]

    barrier = pltpu.get_barrier_semaphore()
    peers = [at(dz=d) for d in range(1, Z)] + [at(dy=d) for d in range(1, Y)]
    peers += [at(dx=dx, core=c if same else other) for dx, same in line]
    for to in peers:
        pl.semaphore_signal(barrier, inc=1, device_id=to, device_id_type=MESH)

    fpad[...] = jnp.zeros_like(fpad)
    fpad[rows(c), :] = feat[...].astype(jnp.float32)
    ft[...] = fpad[...].T.astype(jnp.bfloat16)
    lane = lax.broadcasted_iota(jnp.int32, (SLOTS, BLOCKS), 1)
    col = jnp.sum(jnp.where(lane == sh // 2, cols[0], 0), axis=1, keepdims=True)
    col = (col & (Y - 1)) * Z + (col >> 2)
    meta[pl.ds(COLS_AT, SLOTS), :] = jnp.broadcast_to(col, (SLOTS, TILE))
    count = jnp.sum(jnp.where(lane[0:1] == sh // 2, live[...], 0), axis=1, keepdims=True)
    d = deg[...]
    none = jnp.zeros_like(d)
    meta[0:1, :] = jnp.where(c == 0, jnp.concatenate([d, none], 1), jnp.concatenate([none, d], 1))
    meta[1:2, :] = jnp.broadcast_to(count, (1, TILE))
    pl.semaphore_wait(barrier, len(peers))

    sib = at(core=other)
    send(ft.at[cols_of(2 * x + other)], half_x, h_sem.at[0], h_sem.at[1], sib)

    for q in range(4):
        for dx, k in ((1, q), (-1, 3 - q)):
            send(a_in.at[pl.ds(k * CHUNK, CHUNK)], a_all.at[x, rows(c, k * CHUNK, CHUNK)],
                 as_sem.at[0], a_sem.at[x, k], at(dx=dx))
    send(a_in, a_all.at[x, rows(c)], as_sem.at[2], c_sem.at[x], sib)
    own_a = pltpu.make_async_copy(a_in, a_all.at[x, rows(c)], l_sem.at[0])
    own_a.start()
    for dx, same in line:
        send(meta, mbuf.at[g], ms_sem.at[0], m_sem.at[g], at(dx=dx, core=c if same else other))
    mbuf[g] = meta[...]

    arrived(half_x, h_sem.at[1])
    xg0[blk()] = (ft[cols_of(g), :].astype(jnp.float32) + half_x[...].astype(jnp.float32)).astype(jnp.bfloat16)

    def gather_start(h, src):
        b = blk()
        for dy, dz in DIRECT:
            send(src, xgs[h].at[b], s_sem.at[h], r_sem.at[h, b], at(dy=dy, dz=dz))

    def gather_relay(h):
        for o in RELAYS:
            b = blk(-o[0], -o[1])
            ref = xgs[h].at[b]
            arrived(ref, r_sem.at[h, b])
            for k in KIDS[o]:
                send(ref, ref, s_sem.at[h], r_sem.at[h, b], at(dy=k[0] - o[0], dz=k[1] - o[1]))

    def gather_rest(h):
        for o in LEAVES:
            b = blk(-o[0], -o[1])
            arrived(xgs[h].at[b], r_sem.at[h, b])

    def tile_chunk(s, k):
        ref = a_all.at[s, rows(c, k * CHUNK, CHUNK)]
        arrived(ref, a_sem.at[s, k])
        return ref

    def compute(h):
        for k in range(SLOTS):
            on = (mbuf[2 * h, 1:2, :] > k).astype(jnp.float32).astype(jnp.bfloat16)
            lhs[:, k * TILE:(k + 1) * TILE] = xgs[h][sm[h, k, 0]] * on
        acc = lax.dot_general(lhs[...], a_all[h], (((1,), (1,)), ((), ())),
                              preferred_element_type=jnp.float32)
        degree = mbuf[2 * h, 0:1, :] + mbuf[2 * h + 1, 0:1, :]
        val = (acc * lax.rsqrt(degree.astype(jnp.float32))).astype(jnp.bfloat16)
        ybuf[h] = val
        if h < HOPS - 1:
            xgs[h + 1][blk()] = val
            gather_start(h + 1, ybuf.at[h])

        @pl.when(x == h)
        def _():
            obuf[g] = ybuf[h]
            send(ybuf.at[h], obuf.at[g], os_sem.at[0], o_sem.at[g], sib)

        @pl.when(x != h)
        def _():
            for core in (0, 1):
                send(ybuf.at[h], obuf.at[g], os_sem.at[0], o_sem.at[g], (h, (sh // 2) * 2 + core))

    gather_start(0, xg0.at[blk()])
    gather_relay(0)

    left, right, far = (x - 1) % X, (x + 1) % X, (x + 2) % X
    for q in range(2):
        for s, k, dx in ((left, q, 1), (right, 3 - q, -1)):
            ref = tile_chunk(s, k)
            send(ref, ref, as_sem.at[1], a_sem.at[s, k], at(dx=dx))
    gather_rest(0)
    for dx, same in line:
        p = 2 * ((x + dx) % X) + (c if same else other)
        arrived(mbuf.at[p], m_sem.at[p])
    to_sm = [pltpu.make_async_copy(mbuf.at[2 * s, pl.ds(COLS_AT, SLOTS)], sm.at[s], l_sem.at[1 + s]) for s in range(X)]
    for copy in to_sm:
        copy.start()
    for s, ks in ((left, (2, 3)), (right, (1, 0)), (far, (0, 1, 2, 3))):
        for k in ks:
            tile_chunk(s, k)
        piece = a_all.at[s, rows(c)]
        send(piece, piece, as_sem.at[2], c_sem.at[s], sib)
    own_a.wait()
    for s in range(X):
        arrived(a_all.at[s, rows(other)], c_sem.at[s])
    for copy in to_sm:
        copy.wait()
    compute(0)
    for h in range(1, HOPS):
        gather_relay(h)
        gather_rest(h)
        compute(h)

    for dx, same in line:
        p = 2 * ((x + dx) % X) + (c if same else other)
        arrived(obuf.at[p], o_sem.at[p])
    full = obuf[...].reshape(8 * COLS, TILE).astype(jnp.float32).T
    out[...] = jnp.where(c == 0, full[:HALF], full[HALF:]).astype(jnp.bfloat16)

    arrived(half_x, h_sem.at[0])
    arrived(a_all.at[0], as_sem.at[0])
    arrived(a_all.at[0, pl.ds(0, HALF)], as_sem.at[1])
    arrived(a_all.at[pl.ds(0, 2)], as_sem.at[2])
    arrived(mbuf.at[pl.ds(0, 7)], ms_sem.at[0])
    arrived(obuf.at[pl.ds(0, 7)], os_sem.at[0])
    for h in range(HOPS):
        arrived(xgs[h].at[pl.ds(0, 31)], s_sem.at[h])


def per_device(features, tile_cols, live_tiles, tile_values, degrees):
    a_in = tile_values[0].reshape(HALF, SLOTS * TILE)
    cols = jnp.swapaxes(tile_cols, 1, 2)
    vm = pl.BlockSpec(memory_space=pltpu.VMEM)
    dma = pltpu.SemaphoreType.DMA
    slab = pltpu.VMEM((BLOCKS, COLS, TILE), jnp.bfloat16)
    res = pl.pallas_call(
        kernel,
        out_shape=jax.ShapeDtypeStruct((HALF, 8 * COLS), jnp.bfloat16),
        in_specs=[vm] * 5,
        out_specs=vm,
        scratch_shapes=[
            slab, slab, slab, slab,
            pltpu.VMEM((X, TILE, SLOTS * TILE), jnp.bfloat16),
            pltpu.VMEM((COLS, SLOTS * TILE), jnp.bfloat16),
            pltpu.VMEM((HOPS, COLS, TILE), jnp.bfloat16),
            pltpu.VMEM((COLS, TILE), jnp.bfloat16),
            pltpu.VMEM((TILE, 8 * COLS), jnp.float32),
            pltpu.VMEM((8 * COLS, TILE), jnp.bfloat16),
            pltpu.VMEM((24, TILE), jnp.int32),
            pltpu.VMEM((8, 24, TILE), jnp.int32),
            pltpu.VMEM((8, COLS, TILE), jnp.bfloat16),
            pltpu.SMEM((X, SLOTS, TILE), jnp.int32),
            dma((HOPS, BLOCKS)), dma((HOPS,)), dma((X, 4)), dma((X,)), dma((3,)),
            dma((8,)), dma((1,)), dma((8,)), dma((1,)), dma((2,)), dma((5,)),
        ],
        compiler_params=pltpu.CompilerParams(collective_id=0, has_side_effects=True,
                                             vmem_limit_bytes=40 * 1024 * 1024),
        name="propagate",
    )(features, cols, live_tiles, degrees, a_in)
    return res[None]


def solution(mesh):
    in_specs = (
        P("shard", None),
        P("section", None, None),
        P("section", None),
        P("section", "shard", None, None),
        P("section", "shard"),
    )
    return jax.shard_map(per_device, mesh=mesh, in_specs=in_specs,
                         out_specs=P("section", "shard", None), check_vma=False)
```

time: 88.6 us -> 70 us (0.79)
  Pallas kernels: 83.6 us -> 67.2 us
  other arithmetic: 1.62 us -> 0 us
    pallas_call x1, Pallas kernels: 83.6 us -> 67.2 us  [per_device(): pl.pallas_call(kernel, out_shape=jax.ShapeDtypeStruct((HALF, 8 * COLS), j...]
    dynamic_slice x2 -> x0, local copies, waits for them, and re-layouts: 2.17 us -> none  [the longest x1 1.28 us: per_device(): live = lax.dynamic_index_in_dim(live_tiles[0], row, 0, keepdims=False)]
    unnamed x5 -> x10, local copies, waits for them, and re-layouts: 0.65 us -> 2.34 us
where the time goes in v2:
time: 70 us; the launch traced here: 69.6 us
  Pallas kernels  67.2 us (96%)
  local copies, waits for them, and re-layouts  2.34 us (3%)
    pallas_call x1, Pallas kernels, per_device(): pl.pallas_call(kernel, out_shape=jax.ShapeDtypeStruct((HALF, 8 * COLS), j...  67.2 us
    unnamed x10, local copies, waits for them, and re-layouts  2.34 us

profile of v2, /device:TPU:7, one launch (start us, length us, event | category | flops | bytes accessed | tf_op | source)
XLA Modules:
  0.0 69.6 jit_solution(566737332233454485)
XLA Ops:
  0.0 0.0 copy-start
  0.0 0.0 copy-start.1
  0.0 1.1 %copy.8 = bf16[8,8,16,128]{3,1,2,0:T(8,128)(2,1)S(1)} copy(bf16[8,8,16,128]{3,2,1,0:T(8,128)(2,1)} %bitcast.10) | data formatting | bytes 524288
  1.1 0.0 copy-start.2
  1.1 0.0 copy-start.3
  1.1 0.0 copy-done
  1.1 0.0 copy-done.1
  1.1 0.6 copy-done.2
  1.7 0.0 copy-done.3
  1.7 67.2 %propagate.1 = bf16[64,768]{1,0:T(8,128)(2,1)S(1)} custom-call(bf16[64,768]{1,0:T(8,128)(2,1)S(1)} %copy-done, s32[1,16,32]{2,1,0:T(8,128)S(1)} %bitcast.9, s32[1,32]{1,0:T(1,128)S(1)} %copy-done.2, s32[1,64]{1,0:T(1,128)S(1)} %copy-done.3, bf16[64,2048]{1,0:T(8,128)(2,1)S(1)} %bitcast.7), custom_call_target="tpu_custom_call" | custom-call | tf_op jit(solution)/shard_map/propagate/pallas_call | solution.py:210
  68.9 0.6 copy.10
Async XLA Ops:
  0.0 1.1 %copy-start = (bf16[64,768]{1,0:T(8,128)(2,1)S(1)}, bf16[64,768]{1,0:T(8,128)(2,1)}, u32[]{:S(2)}) copy-start(bf16[64,768]{1,0:T(8,128)(2,1)} %feat.1) | copy-start | bytes 294916
  0.0 1.1 %copy-start.1 = (s32[1,32,16]{1,2,0:T(8,128)S(1)}, s32[1,32,16]{1,2,0:T(8,128)}, u32[]{:S(2)}) copy-start(s32[1,32,16]{1,2,0:T(8,128)} %param.6) | copy-start | bytes 6148
  1.1 0.7 copy-start.2
  1.1 0.7 copy-start.3

commit v3 on v2

--- a/solution.py
+++ b/solution.py
@@ -78,21 +78,15 @@
         pl.semaphore_signal(barrier, inc=1, device_id=to, device_id_type=MESH)
 
     fpad[...] = jnp.zeros_like(fpad)
-    fpad[rows(c), :] = feat[...].astype(jnp.float32)
+    for i in range(X):
+        @pl.when(x == i)
+        def _():
+            fpad[rows(c), :] = feat[:, 2 * COLS * i:2 * COLS * (i + 1)].astype(jnp.float32)
     ft[...] = fpad[...].T.astype(jnp.bfloat16)
-    lane = lax.broadcasted_iota(jnp.int32, (SLOTS, BLOCKS), 1)
-    col = jnp.sum(jnp.where(lane == sh // 2, cols[0], 0), axis=1, keepdims=True)
-    col = (col & (Y - 1)) * Z + (col >> 2)
-    meta[pl.ds(COLS_AT, SLOTS), :] = jnp.broadcast_to(col, (SLOTS, TILE))
-    count = jnp.sum(jnp.where(lane[0:1] == sh // 2, live[...], 0), axis=1, keepdims=True)
-    d = deg[...]
-    none = jnp.zeros_like(d)
-    meta[0:1, :] = jnp.where(c == 0, jnp.concatenate([d, none], 1), jnp.concatenate([none, d], 1))
-    meta[1:2, :] = jnp.broadcast_to(count, (1, TILE))
     pl.semaphore_wait(barrier, len(peers))
 
     sib = at(core=other)
-    send(ft.at[cols_of(2 * x + other)], half_x, h_sem.at[0], h_sem.at[1], sib)
+    send(ft.at[cols_of(other)], half_x, h_sem.at[0], h_sem.at[1], sib)
 
     for q in range(4):
         for dx, k in ((1, q), (-1, 3 - q)):
@@ -101,13 +95,6 @@
     send(a_in, a_all.at[x, rows(c)], as_sem.at[2], c_sem.at[x], sib)
     own_a = pltpu.make_async_copy(a_in, a_all.at[x, rows(c)], l_sem.at[0])
     own_a.start()
-    for dx, same in line:
-        send(meta, mbuf.at[g], ms_sem.at[0], m_sem.at[g], at(dx=dx, core=c if same else other))
-    mbuf[g] = meta[...]
-
-    arrived(half_x, h_sem.at[1])
-    xg0[blk()] = (ft[cols_of(g), :].astype(jnp.float32) + half_x[...].astype(jnp.float32)).astype(jnp.bfloat16)
-
     def gather_start(h, src):
         b = blk()
         for dy, dz in DIRECT:
@@ -154,35 +141,47 @@
             for core in (0, 1):
                 send(ybuf.at[h], obuf.at[g], os_sem.at[0], o_sem.at[g], (h, (sh // 2) * 2 + core))
 
+    arrived(half_x, h_sem.at[1])
+    xg0[blk()] = (ft[cols_of(c), :].astype(jnp.float32) + half_x[...].astype(jnp.float32)).astype(jnp.bfloat16)
     gather_start(0, xg0.at[blk()])
+    lane = lax.broadcasted_iota(jnp.int32, (SLOTS, BLOCKS), 1)
+    col = jnp.sum(jnp.where(lane == sh // 2, cols[0], 0), axis=1, keepdims=True)
+    col = (col & (Y - 1)) * Z + (col >> 2)
+    meta[pl.ds(COLS_AT, SLOTS), :] = jnp.broadcast_to(col, (SLOTS, TILE))
+    count = jnp.sum(jnp.where(lane[0:1] == sh // 2, live[...], 0), axis=1, keepdims=True)
+    d = deg[...]
+    none = jnp.zeros_like(d)
+    meta[0:1, :] = jnp.where(c == 0, jnp.concatenate([d, none], 1), jnp.concatenate([none, d], 1))
+    meta[1:2, :] = jnp.broadcast_to(count, (1, TILE))
+    for dx, same in line:
+        send(meta, mbuf.at[g], ms_sem.at[0], m_sem.at[g], at(dx=dx, core=c if same else other))
+    mbuf[g] = meta[...]
     gather_relay(0)
 
-    left, right, far = (x - 1) % X, (x + 1) % X, (x + 2) % X
+    left, right, far_x = (x - 1) % X, (x + 1) % X, (x + 2) % X
     for q in range(2):
         for s, k, dx in ((left, q, 1), (right, 3 - q, -1)):
             ref = tile_chunk(s, k)
             send(ref, ref, as_sem.at[1], a_sem.at[s, k], at(dx=dx))
-    gather_rest(0)
+    for s, ks in ((left, (2, 3)), (right, (1, 0)), (far_x, (0, 1, 2, 3))):
+        for k in ks:
+            tile_chunk(s, k)
+        piece = a_all.at[s, rows(c)]
+        send(piece, piece, as_sem.at[2], c_sem.at[s], sib)
     for dx, same in line:
         p = 2 * ((x + dx) % X) + (c if same else other)
         arrived(mbuf.at[p], m_sem.at[p])
     to_sm = [pltpu.make_async_copy(mbuf.at[2 * s, pl.ds(COLS_AT, SLOTS)], sm.at[s], l_sem.at[1 + s]) for s in range(X)]
     for copy in to_sm:
         copy.start()
-    for s, ks in ((left, (2, 3)), (right, (1, 0)), (far, (0, 1, 2, 3))):
-        for k in ks:
-            tile_chunk(s, k)
-        piece = a_all.at[s, rows(c)]
-        send(piece, piece, as_sem.at[2], c_sem.at[s], sib)
     own_a.wait()
-    for s in range(X):
-        arrived(a_all.at[s, rows(other)], c_sem.at[s])
     for copy in to_sm:
         copy.wait()
-    compute(0)
-    for h in range(1, HOPS):
-        gather_relay(h)
+    for h in range(HOPS):
+        if h:
+            gather_relay(h)
         gather_rest(h)
+        arrived(a_all.at[h, rows(other)], c_sem.at[h])
         compute(h)
 
     for dx, same in line:
@@ -218,8 +217,8 @@
             pltpu.VMEM((COLS, SLOTS * TILE), jnp.bfloat16),
             pltpu.VMEM((HOPS, COLS, TILE), jnp.bfloat16),
             pltpu.VMEM((COLS, TILE), jnp.bfloat16),
-            pltpu.VMEM((TILE, 8 * COLS), jnp.float32),
-            pltpu.VMEM((8 * COLS, TILE), jnp.bfloat16),
+            pltpu.VMEM((TILE, 2 * COLS), jnp.float32),
+            pltpu.VMEM((2 * COLS, TILE), jnp.bfloat16),
             pltpu.VMEM((24, TILE), jnp.int32),
             pltpu.VMEM((8, 24, TILE), jnp.int32),
             pltpu.VMEM((8, COLS, TILE), jnp.bfloat16),

time: 70 us -> 67.1 us (0.959)
  Pallas kernels: 67.2 us -> 64.6 us
    pallas_call x1, Pallas kernels: 67.2 us -> 64.6 us  [per_device(): pl.pallas_call(kernel, out_shape=jax.ShapeDtypeStruct((HALF, 8 * COLS), j...]
where the time goes in v3:
time: 67.1 us; the launch traced here: 67 us
  Pallas kernels  64.6 us (96%)
  local copies, waits for them, and re-layouts  2.34 us (3%)
    pallas_call x1, Pallas kernels, per_device(): pl.pallas_call(kernel, out_shape=jax.ShapeDtypeStruct((HALF, 8 * COLS), j...  64.6 us
    unnamed x10, local copies, waits for them, and re-layouts  2.34 us

profile of v3, /device:TPU:7, one launch (start us, length us, event | category | flops | bytes accessed | tf_op | source)
XLA Modules:
  0.0 67.0 jit_solution(1622028874818682145)
XLA Ops:
  0.0 0.0 copy-start
  0.0 0.0 copy-start.1
  0.0 1.1 %copy.8 = bf16[8,8,16,128]{3,1,2,0:T(8,128)(2,1)S(1)} copy(bf16[8,8,16,128]{3,2,1,0:T(8,128)(2,1)} %bitcast.10) | data formatting | bytes 524288
  1.1 0.0 copy-start.2
  1.1 0.0 copy-start.3
  1.1 0.0 copy-done
  1.1 0.0 copy-done.1
  1.1 0.6 copy-done.2
  1.7 0.0 copy-done.3
  1.7 64.6 %propagate.1 = bf16[64,768]{1,0:T(8,128)(2,1)S(1)} custom-call(bf16[64,768]{1,0:T(8,128)(2,1)S(1)} %copy-done, s32[1,16,32]{2,1,0:T(8,128)S(1)} %bitcast.9, s32[1,32]{1,0:T(1,128)S(1)} %copy-done.2, s32[1,64]{1,0:T(1,128)S(1)} %copy-done.3, bf16[64,2048]{1,0:T(8,128)(2,1)S(1)} %bitcast.7), custom_call_target="tpu_custom_call" | custom-call | tf_op jit(solution)/shard_map/propagate/pallas_call | solution.py:209
  66.3 0.6 copy.10
Async XLA Ops:
  0.0 1.1 %copy-start = (bf16[64,768]{1,0:T(8,128)(2,1)S(1)}, bf16[64,768]{1,0:T(8,128)(2,1)}, u32[]{:S(2)}) copy-start(bf16[64,768]{1,0:T(8,128)(2,1)} %feat.1) | copy-start | bytes 294916
  0.0 1.1 %copy-start.1 = (s32[1,32,16]{1,2,0:T(8,128)S(1)}, s32[1,32,16]{1,2,0:T(8,128)}, u32[]{:S(2)}) copy-start(s32[1,32,16]{1,2,0:T(8,128)} %param.6) | copy-start | bytes 6148
  1.1 0.7 copy-start.2
  1.1 0.7 copy-start.3

commit v4 on v3

v4 whole, which is shorter than its diff:
```python
import jax
import jax.numpy as jnp
from jax import lax
from jax.experimental import pallas as pl
from jax.experimental.pallas import tpu as pltpu
from jax.sharding import PartitionSpec as P

MESH = pl.DeviceIdType.MESH
X, Y, Z = 4, 4, 8
HOPS = 4
TILE = 128
SLOTS = 16
BLOCKS = Y * Z
HALF = 64
CHUNK = 16
CHIP = 192
WIDTH = (64, 128)
FIRST = (0, 64)
COLS_AT = 8
DYS = (0, 1, -1, 2)
DZS = (0, 1, -1, 2, -2, 3, -3, 4)


def parent(dy, dz):
    if dy == 0 or dz == 0:
        return (0, 0)
    if abs(dz) <= 2:
        return (dy, 0)
    return (0, dz)


def far(o):
    return abs(o[0]) + abs(o[1])


OFFSETS = [(dy, dz) for dz in DZS for dy in DYS if dy or dz]
KIDS = {}
for _o in sorted(OFFSETS, key=lambda o: -far(o)):
    KIDS.setdefault(parent(*_o), []).append(_o)
DIRECT = sorted(KIDS.pop((0, 0)), key=lambda o: (o not in KIDS, -far(o)))
RELAYS = sorted(KIDS, key=far)
LEAVES = [o for o in sorted(OFFSETS, key=lambda o: (far(o) + far(parent(*o)), far(o))) if o not in KIDS]


def send(src, dst, ssem, rsem, to):
    pltpu.make_async_remote_copy(src_ref=src, dst_ref=dst, send_sem=ssem, recv_sem=rsem,
                                 device_id=to, device_id_type=MESH).start()


def arrived(ref, sem):
    pltpu.make_async_copy(ref, ref, sem).wait()


def kernel(*refs):
    core = lax.axis_index("shard") % 2
    for c in (0, 1):
        @pl.when(core == c)
        def _():
            run(c, *refs)


def run(c, feat, cols, live, deg, a_in, out, xg0, xg1, xg2, xg3, a_all, lhs, ybuf, tbuf, half_x, ft, meta, mbuf, obuf, sm,
        r_sem, s_sem, a_sem, c_sem, as_sem, m_sem, ms_sem, o_sem, os_sem, h_sem, l_sem):
    x = lax.axis_index("section")
    sh = lax.axis_index("shard")
    z, y = sh // 8, (sh // 2) % 4
    g = 2 * x + c
    xgs = (xg0, xg1, xg2, xg3)
    other = 1 - c
    w = WIDTH[c]
    mine, theirs = pl.ds(FIRST[c], w), pl.ds(FIRST[other], WIDTH[other])

    def at(dx=0, dy=0, dz=0, core=c):
        return ((x + dx) % X, ((z + dz) % Z) * 8 + ((y + dy) % Y) * 2 + core)

    def blk(dy=0, dz=0):
        return ((y + dy) % Y) * Z + (z + dz) % Z

    def block(h, b):
        return xgs[h].at[b, pl.ds(0, w)]

    def rows(core, first=0, count=HALF):
        return pl.ds(core * HALF + first, count)

    line = [(dx, core) for dx in range(X) for core in (c, other) if (dx, core) != (0, c)]
    sib = at(core=other)

    barrier = pltpu.get_barrier_semaphore()
    peers = [at(dz=d) for d in range(1, Z)] + [at(dy=d) for d in range(1, Y)]
    peers += [at(dx=dx, core=core) for dx, core in line]
    for to in peers:
        pl.semaphore_signal(barrier, inc=1, device_id=to, device_id_type=MESH)

    for i in range(X):
        @pl.when(x == i)
        def _():
            part = feat[:, CHIP * i:CHIP * (i + 1)].astype(jnp.float32)
            none = jnp.zeros_like(part)
            ft[...] = jnp.concatenate([part, none] if c == 0 else [none, part], 0).T.astype(jnp.bfloat16)
    pl.semaphore_wait(barrier, len(peers))

    send(ft.at[theirs], half_x.at[pl.ds(0, WIDTH[other])], h_sem.at[0], h_sem.at[1], sib)

    for q in range(4):
        for dx, k in ((1, q), (-1, 3 - q)):
            send(a_in.at[pl.ds(k * CHUNK, CHUNK)], a_all.at[x, rows(c, k * CHUNK, CHUNK)],
                 as_sem.at[0], a_sem.at[x, k], at(dx=dx))
    send(a_in, a_all.at[x, rows(c)], as_sem.at[2], c_sem.at[x], sib)
    own_a = pltpu.make_async_copy(a_in, a_all.at[x, rows(c)], l_sem.at[0])
    own_a.start()

    def gather_start(h, src):
        b = blk()
        for dy, dz in DIRECT:
            send(src, block(h, b), s_sem.at[h], r_sem.at[h, b], at(dy=dy, dz=dz))

    def gather_relay(h):
        for o in RELAYS:
            b = blk(-o[0], -o[1])
            ref = block(h, b)
            arrived(ref, r_sem.at[h, b])
            for k in KIDS[o]:
                send(ref, ref, s_sem.at[h], r_sem.at[h, b], at(dy=k[0] - o[0], dz=k[1] - o[1]))

    def gather_rest(h):
        for o in LEAVES:
            b = blk(-o[0], -o[1])
            arrived(block(h, b), r_sem.at[h, b])

    def tile_chunk(s, k):
        ref = a_all.at[s, rows(c, k * CHUNK, CHUNK)]
        arrived(ref, a_sem.at[s, k])
        return ref

    def compute(h):
        for k in range(SLOTS):
            on = (mbuf[2 * h, 1:2, :] > k).astype(jnp.float32).astype(jnp.bfloat16)
            lhs[0:w, k * TILE:(k + 1) * TILE] = xgs[h][sm[h, k, 0], 0:w] * on
        acc = lax.dot_general(lhs[0:w, :], a_all[h], (((1,), (1,)), ((), ())),
                              preferred_element_type=jnp.float32)
        degree = mbuf[2 * h, 0:1, :] + mbuf[2 * h + 1, 0:1, :]
        val = acc * lax.rsqrt(degree.astype(jnp.float32))
        if h < HOPS - 1:
            ybuf[h, 0:w] = val.astype(jnp.bfloat16)
            xgs[h + 1][blk(), 0:w] = val.astype(jnp.bfloat16)
            gather_start(h + 1, ybuf.at[h, pl.ds(0, w)])
        wide = jnp.concatenate([val, val], 0) if w == HALF else val
        tbuf[h] = wide.T.astype(jnp.bfloat16)

        @pl.when(x == h)
        def _():
            obuf[g] = tbuf[h, c * HALF:(c + 1) * HALF]
            send(tbuf.at[h, rows(other)], obuf.at[g], os_sem.at[0], o_sem.at[g], sib)

        @pl.when(x != h)
        def _():
            for core in (0, 1):
                send(tbuf.at[h, rows(core)], obuf.at[g], os_sem.at[0], o_sem.at[g], (h, (sh // 2) * 2 + core))

    arrived(half_x.at[pl.ds(0, w)], h_sem.at[1])
    xg0[blk(), 0:w] = (ft[FIRST[c]:FIRST[c] + w].astype(jnp.float32) + half_x[0:w].astype(jnp.float32)).astype(jnp.bfloat16)
    gather_start(0, block(0, blk()))
    lane = lax.broadcasted_iota(jnp.int32, (SLOTS, BLOCKS), 1)
    col = jnp.sum(jnp.where(lane == sh // 2, cols[0], 0), axis=1, keepdims=True)
    col = (col & (Y - 1)) * Z + (col >> 2)
    meta[pl.ds(COLS_AT, SLOTS), :] = jnp.broadcast_to(col, (SLOTS, TILE))
    count = jnp.sum(jnp.where(lane[0:1] == sh // 2, live[...], 0), axis=1, keepdims=True)
    d = deg[...]
    none = jnp.zeros_like(d)
    meta[0:1, :] = jnp.concatenate([d, none] if c == 0 else [none, d], 1)
    meta[1:2, :] = jnp.broadcast_to(count, (1, TILE))
    for dx, core in line:
        send(meta, mbuf.at[g], ms_sem.at[0], m_sem.at[g], at(dx=dx, core=core))
    mbuf[g] = meta[...]
    gather_relay(0)

    left, right, far_x = (x - 1) % X, (x + 1) % X, (x + 2) % X
    for q in range(2):
        for s, k, dx in ((left, q, 1), (right, 3 - q, -1)):
            ref = tile_chunk(s, k)
            send(ref, ref, as_sem.at[1], a_sem.at[s, k], at(dx=dx))
    for s, ks in ((left, (2, 3)), (right, (1, 0)), (far_x, (0, 1, 2, 3))):
        for k in ks:
            tile_chunk(s, k)
        piece = a_all.at[s, rows(c)]
        send(piece, piece, as_sem.at[2], c_sem.at[s], sib)
    for dx, core in line:
        p = 2 * ((x + dx) % X) + core
        arrived(mbuf.at[p], m_sem.at[p])
    to_sm = [pltpu.make_async_copy(mbuf.at[2 * s, pl.ds(COLS_AT, SLOTS)], sm.at[s], l_sem.at[1 + s]) for s in range(X)]
    for copy in to_sm:
        copy.start()
    own_a.wait()
    for copy in to_sm:
        copy.wait()
    for h in range(HOPS):
        if h:
            gather_relay(h)
        gather_rest(h)
        arrived(a_all.at[h, rows(other)], c_sem.at[h])
        compute(h)

    for dx, core in line:
        p = 2 * ((x + dx) % X) + core
        arrived(obuf.at[p], o_sem.at[p])
    low = lax.broadcasted_iota(jnp.int32, (HALF, TILE), 1) < HALF
    for i in range(0, X, 2):
        p0, p1, q0, q1 = (obuf[2 * i + j].astype(jnp.float32) for j in range(4))
        turned = jnp.concatenate([p1[:, HALF:], p1[:, :HALF]], 1)
        at0 = CHIP * i
        out[:, at0:at0 + TILE] = jnp.where(low, p0, turned).astype(jnp.bfloat16)
        out[:, at0 + TILE:at0 + 2 * TILE] = jnp.where(low, turned, q0).astype(jnp.bfloat16)
        out[:, at0 + 2 * TILE:at0 + 3 * TILE] = q1.astype(jnp.bfloat16)

    arrived(half_x.at[pl.ds(0, WIDTH[other])], h_sem.at[0])
    arrived(a_all.at[0], as_sem.at[0])
    arrived(a_all.at[0, pl.ds(0, HALF)], as_sem.at[1])
    arrived(a_all.at[pl.ds(0, 2)], as_sem.at[2])
    arrived(mbuf.at[pl.ds(0, 7)], ms_sem.at[0])
    arrived(obuf.at[pl.ds(0, 7)], os_sem.at[0])
    for h in range(HOPS):
        arrived(xgs[h].at[pl.ds(0, 31), pl.ds(0, w)], s_sem.at[h])


def per_device(features, tile_cols, live_tiles, tile_values, degrees):
    a_in = tile_values[0].reshape(HALF, SLOTS * TILE)
    cols = jnp.swapaxes(tile_cols, 1, 2)
    vm = pl.BlockSpec(memory_space=pltpu.VMEM)
    dma = pltpu.SemaphoreType.DMA
    slab = pltpu.VMEM((BLOCKS, TILE, TILE), jnp.bfloat16)
    res = pl.pallas_call(
        kernel,
        out_shape=jax.ShapeDtypeStruct((HALF, X * CHIP), jnp.bfloat16),
        in_specs=[vm] * 5,
        out_specs=vm,
        scratch_shapes=[
            slab, slab, slab, slab,
            pltpu.VMEM((X, TILE, SLOTS * TILE), jnp.bfloat16),
            pltpu.VMEM((TILE, SLOTS * TILE), jnp.bfloat16),
            pltpu.VMEM((HOPS, TILE, TILE), jnp.bfloat16),
            pltpu.VMEM((HOPS, TILE, TILE), jnp.bfloat16),
            pltpu.VMEM((TILE, TILE), jnp.bfloat16),
            pltpu.VMEM((CHIP, TILE), jnp.bfloat16),
            pltpu.VMEM((24, TILE), jnp.int32),
            pltpu.VMEM((8, 24, TILE), jnp.int32),
            pltpu.VMEM((8, HALF, TILE), jnp.bfloat16),
            pltpu.SMEM((X, SLOTS, TILE), jnp.int32),
            dma((HOPS, BLOCKS)), dma((HOPS,)), dma((X, 4)), dma((X,)), dma((3,)),
            dma((8,)), dma((1,)), dma((8,)), dma((1,)), dma((2,)), dma((5,)),
        ],
        compiler_params=pltpu.CompilerParams(collective_id=0, has_side_effects=True,
                                             vmem_limit_bytes=40 * 1024 * 1024),
        name="propagate",
    )(features, cols, live_tiles, degrees, a_in)
    return res[None]


def solution(mesh):
    in_specs = (
        P("shard", None),
        P("section", None, None),
        P("section", None),
        P("section", "shard", None, None),
        P("section", "shard"),
    )
    return jax.shard_map(per_device, mesh=mesh, in_specs=in_specs,
                         out_specs=P("section", "shard", None), check_vma=False)
```

time: 67.1 us -> 63.4 us (0.945)
  Pallas kernels: 64.6 us -> 60.9 us
    pallas_call x1, Pallas kernels: 64.6 us -> 60.9 us  [per_device(): pl.pallas_call(kernel, out_shape=jax.ShapeDtypeStruct((HALF, X * CHIP), j...]
where the time goes in v4:
time: 63.4 us; the launch traced here: 63.3 us
  Pallas kernels  60.9 us (96%)
  local copies, waits for them, and re-layouts  2.34 us (4%)
    pallas_call x1, Pallas kernels, per_device(): pl.pallas_call(kernel, out_shape=jax.ShapeDtypeStruct((HALF, X * CHIP), j...  60.9 us
    unnamed x10, local copies, waits for them, and re-layouts  2.34 us

profile of v4, /device:TPU:7, one launch (start us, length us, event | category | flops | bytes accessed | tf_op | source)
XLA Modules:
  0.0 63.3 jit_solution(2197958721565568879)
XLA Ops:
  0.0 0.0 copy-start
  0.0 0.0 copy-start.1
  0.0 1.1 %copy.8 = bf16[8,8,16,128]{3,1,2,0:T(8,128)(2,1)S(1)} copy(bf16[8,8,16,128]{3,2,1,0:T(8,128)(2,1)} %bitcast.10) | data formatting | bytes 524288
  1.1 0.0 copy-start.2
  1.1 0.0 copy-start.3
  1.1 0.0 copy-done
  1.1 0.0 copy-done.1
  1.1 0.6 copy-done.2
  1.7 0.0 copy-done.3
  1.7 60.9 %propagate.1 = bf16[64,768]{1,0:T(8,128)(2,1)S(1)} custom-call(bf16[64,768]{1,0:T(8,128)(2,1)S(1)} %copy-done, s32[1,16,32]{2,1,0:T(8,128)S(1)} %bitcast.9, s32[1,32]{1,0:T(1,128)S(1)} %copy-done.2, s32[1,64]{1,0:T(1,128)S(1)} %copy-done.3, bf16[64,2048]{1,0:T(8,128)(2,1)S(1)} %bitcast.7), custom_call_target="tpu_custom_call" | custom-call | tf_op jit(solution)/shard_map/propagate/pallas_call | solution.py:231
  62.6 0.6 %copy.10 = bf16[1,64,768]{2,1,0:T(8,128)(2,1)} copy(bf16[1,64,768]{2,1,0:T(8,128)(2,1)S(1)} %bitcast.8) | data formatting | bytes 196608
Async XLA Ops:
  0.0 1.1 %copy-start = (bf16[64,768]{1,0:T(8,128)(2,1)S(1)}, bf16[64,768]{1,0:T(8,128)(2,1)}, u32[]{:S(2)}) copy-start(bf16[64,768]{1,0:T(8,128)(2,1)} %refs_0_.1) | copy-start | bytes 294916
  0.0 1.1 %copy-start.1 = (s32[1,32,16]{1,2,0:T(8,128)S(1)}, s32[1,32,16]{1,2,0:T(8,128)}, u32[]{:S(2)}) copy-start(s32[1,32,16]{1,2,0:T(8,128)} %param.6) | copy-start | bytes 6148
  1.1 0.7 %copy-start.2 = (s32[1,32]{1,0:T(1,128)S(1)}, s32[1,32]{1,0:T(1,128)}, u32[]{:S(2)}) copy-start(s32[1,32]{1,0:T(1,128)} %refs_2_.1) | copy-start | bytes 388
  1.1 0.7 %copy-start.3 = (s32[1,64]{1,0:T(1,128)S(1)}, s32[1,64]{1,0:T(1,128)}, u32[]{:S(2)}) copy-start(s32[1,64]{1,0:T(1,128)} %refs_3_.1) | copy-start | bytes 772

commit v5 on v4

--- a/solution.py
+++ b/solution.py
@@ -24,7 +24,7 @@
 def parent(dy, dz):
     if dy == 0 or dz == 0:
         return (0, 0)
-    if abs(dz) <= 2:
+    if abs(dz) == 1 or (abs(dz) == 2 and dy == 2):
         return (dy, 0)
     return (0, dz)
 

time: 63.4 us -> 67 us (1.057)
  Pallas kernels: 60.9 us -> 64.4 us
    pallas_call x1, Pallas kernels: 60.9 us -> 64.4 us  [per_device(): pl.pallas_call(kernel, out_shape=jax.ShapeDtypeStruct((HALF, X * CHIP), j...]
where the time goes in v5:
time: 67 us; the launch traced here: 66.7 us
  Pallas kernels  64.4 us (96%)
  local copies, waits for them, and re-layouts  2.34 us (3%)
    pallas_call x1, Pallas kernels, per_device(): pl.pallas_call(kernel, out_shape=jax.ShapeDtypeStruct((HALF, X * CHIP), j...  64.4 us
    unnamed x10, local copies, waits for them, and re-layouts  2.34 us

profile of v5, /device:TPU:7, one launch (start us, length us, event | category | flops | bytes accessed | tf_op | source)
XLA Modules:
  0.0 66.7 jit_solution(16602409392356414701)
XLA Ops:
  0.0 0.0 copy-start
  0.0 0.0 copy-start.1
  0.0 1.1 %copy.8 = bf16[8,8,16,128]{3,1,2,0:T(8,128)(2,1)S(1)} copy(bf16[8,8,16,128]{3,2,1,0:T(8,128)(2,1)} %bitcast.10) | data formatting | bytes 524288
  1.1 0.0 copy-start.2
  1.1 0.0 copy-start.3
  1.1 0.0 copy-done
  1.1 0.0 copy-done.1
  1.1 0.6 copy-done.2
  1.7 0.0 copy-done.3
  1.7 64.4 %propagate.1 = bf16[64,768]{1,0:T(8,128)(2,1)S(1)} custom-call(bf16[64,768]{1,0:T(8,128)(2,1)S(1)} %copy-done, s32[1,16,32]{2,1,0:T(8,128)S(1)} %bitcast.9, s32[1,32]{1,0:T(1,128)S(1)} %copy-done.2, s32[1,64]{1,0:T(1,128)S(1)} %copy-done.3, bf16[64,2048]{1,0:T(8,128)(2,1)S(1)} %bitcast.7), custom_call_target="tpu_custom_call" | custom-call | tf_op jit(solution)/shard_map/propagate/pallas_call | solution.py:231
  66.1 0.6 copy.10
Async XLA Ops:
  0.0 1.1 %copy-start = (bf16[64,768]{1,0:T(8,128)(2,1)S(1)}, bf16[64,768]{1,0:T(8,128)(2,1)}, u32[]{:S(2)}) copy-start(bf16[64,768]{1,0:T(8,128)(2,1)} %refs_0_.1) | copy-start | bytes 294916
  0.0 1.1 %copy-start.1 = (s32[1,32,16]{1,2,0:T(8,128)S(1)}, s32[1,32,16]{1,2,0:T(8,128)}, u32[]{:S(2)}) copy-start(s32[1,32,16]{1,2,0:T(8,128)} %param.6) | copy-start | bytes 6148
  1.1 0.7 copy-start.2
  1.1 0.7 copy-start.3

commit v6 on v4

--- a/solution.py
+++ b/solution.py
@@ -59,7 +59,7 @@
             run(c, *refs)
 
 
-def run(c, feat, cols, live, deg, a_in, out, xg0, xg1, xg2, xg3, a_all, lhs, ybuf, tbuf, half_x, ft, meta, mbuf, obuf, sm,
+def run(c, feat, cols, live, deg, a_in, out, xg0, xg1, xg2, xg3, a_all, ybuf, tbuf, half_x, ft, meta, mbuf, obuf, a_t, sm,
         r_sem, s_sem, a_sem, c_sem, as_sem, m_sem, ms_sem, o_sem, os_sem, h_sem, l_sem):
     x = lax.axis_index("section")
     sh = lax.axis_index("shard")
@@ -114,8 +114,8 @@
         for dy, dz in DIRECT:
             send(src, block(h, b), s_sem.at[h], r_sem.at[h, b], at(dy=dy, dz=dz))
 
-    def gather_relay(h):
-        for o in RELAYS:
+    def gather_relay(h, relays=RELAYS):
+        for o in relays:
             b = blk(-o[0], -o[1])
             ref = block(h, b)
             arrived(ref, r_sem.at[h, b])
@@ -132,14 +132,20 @@
         arrived(ref, a_sem.at[s, k])
         return ref
 
-    def compute(h):
+    def prepare(h):
+        a_t[...] = a_all[h].T
         for k in range(SLOTS):
             on = (mbuf[2 * h, 1:2, :] > k).astype(jnp.float32).astype(jnp.bfloat16)
-            lhs[0:w, k * TILE:(k + 1) * TILE] = xgs[h][sm[h, k, 0], 0:w] * on
-        acc = lax.dot_general(lhs[0:w, :], a_all[h], (((1,), (1,)), ((), ())),
-                              preferred_element_type=jnp.float32)
+            a_t[k * TILE:(k + 1) * TILE, :] = a_t[k * TILE:(k + 1) * TILE, :] * on
         degree = mbuf[2 * h, 0:1, :] + mbuf[2 * h + 1, 0:1, :]
-        val = acc * lax.rsqrt(degree.astype(jnp.float32))
+        return lax.rsqrt(degree.astype(jnp.float32))
+
+    def compute(h, scale):
+        acc = jnp.zeros((w, TILE), jnp.float32)
+        for k in range(0, SLOTS, 4):
+            src = jnp.concatenate([xgs[h][sm[h, k + i, 0], 0:w] for i in range(4)], axis=1)
+            acc = acc + jnp.dot(src, a_t[k * TILE:(k + 4) * TILE, :], preferred_element_type=jnp.float32)
+        val = acc * scale
         if h < HOPS - 1:
             ybuf[h, 0:w] = val.astype(jnp.bfloat16)
             xgs[h + 1][blk(), 0:w] = val.astype(jnp.bfloat16)
@@ -172,13 +178,15 @@
     for dx, core in line:
         send(meta, mbuf.at[g], ms_sem.at[0], m_sem.at[g], at(dx=dx, core=core))
     mbuf[g] = meta[...]
-    gather_relay(0)
+    gather_relay(0, RELAYS[:3])
 
     left, right, far_x = (x - 1) % X, (x + 1) % X, (x + 2) % X
     for q in range(2):
         for s, k, dx in ((left, q, 1), (right, 3 - q, -1)):
             ref = tile_chunk(s, k)
             send(ref, ref, as_sem.at[1], a_sem.at[s, k], at(dx=dx))
+    gather_relay(0, RELAYS[3:])
+
     for s, ks in ((left, (2, 3)), (right, (1, 0)), (far_x, (0, 1, 2, 3))):
         for k in ks:
             tile_chunk(s, k)
@@ -196,9 +204,10 @@
     for h in range(HOPS):
         if h:
             gather_relay(h)
+        arrived(a_all.at[h, rows(other)], c_sem.at[h])
+        scale = prepare(h)
         gather_rest(h)
-        arrived(a_all.at[h, rows(other)], c_sem.at[h])
-        compute(h)
+        compute(h, scale)
 
     for dx, core in line:
         p = 2 * ((x + dx) % X) + core
@@ -236,7 +245,6 @@
         scratch_shapes=[
             slab, slab, slab, slab,
             pltpu.VMEM((X, TILE, SLOTS * TILE), jnp.bfloat16),
-            pltpu.VMEM((TILE, SLOTS * TILE), jnp.bfloat16),
             pltpu.VMEM((HOPS, TILE, TILE), jnp.bfloat16),
             pltpu.VMEM((HOPS, TILE, TILE), jnp.bfloat16),
             pltpu.VMEM((TILE, TILE), jnp.bfloat16),
@@ -244,6 +252,7 @@
             pltpu.VMEM((24, TILE), jnp.int32),
             pltpu.VMEM((8, 24, TILE), jnp.int32),
             pltpu.VMEM((8, HALF, TILE), jnp.bfloat16),
+            pltpu.VMEM((SLOTS * TILE, TILE), jnp.bfloat16),
             pltpu.SMEM((X, SLOTS, TILE), jnp.int32),
             dma((HOPS, BLOCKS)), dma((HOPS,)), dma((X, 4)), dma((X,)), dma((3,)),
             dma((8,)), dma((1,)), dma((8,)), dma((1,)), dma((2,)), dma((5,)),

time: 63.4 us -> 62.7 us (0.989)
  no operation moved by 1% of the time
where the time goes in v6:
time: 62.7 us; the launch traced here: 62.6 us
  Pallas kernels  60.3 us (96%)
  local copies, waits for them, and re-layouts  2.34 us (4%)
    pallas_call x1, Pallas kernels, per_device(): pl.pallas_call(kernel, out_shape=jax.ShapeDtypeStruct((HALF, X * CHIP), j...  60.3 us
    unnamed x10, local copies, waits for them, and re-layouts  2.34 us

profile of v6, /device:TPU:7, one launch (start us, length us, event | category | flops | bytes accessed | tf_op | source)
XLA Modules:
  0.0 62.6 jit_solution(7033698977385604347)
XLA Ops:
  0.0 0.0 copy-start
  0.0 0.0 copy-start.1
  0.0 1.1 %copy.8 = bf16[8,8,16,128]{3,1,2,0:T(8,128)(2,1)S(1)} copy(bf16[8,8,16,128]{3,2,1,0:T(8,128)(2,1)} %bitcast.10) | data formatting | bytes 524288
  1.1 0.0 copy-start.2
  1.1 0.0 copy-start.3
  1.1 0.0 copy-done
  1.1 0.0 copy-done.1
  1.1 0.6 copy-done.2
  1.7 0.0 copy-done.3
  1.7 60.3 %propagate.1 = bf16[64,768]{1,0:T(8,128)(2,1)S(1)} custom-call(bf16[64,768]{1,0:T(8,128)(2,1)S(1)} %copy-done, s32[1,16,32]{2,1,0:T(8,128)S(1)} %bitcast.9, s32[1,32]{1,0:T(1,128)S(1)} %copy-done.2, s32[1,64]{1,0:T(1,128)S(1)} %copy-done.3, bf16[64,2048]{1,0:T(8,128)(2,1)S(1)} %bitcast.7), custom_call_target="tpu_custom_call" | custom-call | tf_op jit(solution)/shard_map/propagate/pallas_call | solution.py:240
  62.0 0.6 %copy.10 = bf16[1,64,768]{2,1,0:T(8,128)(2,1)} copy(bf16[1,64,768]{2,1,0:T(8,128)(2,1)S(1)} %bitcast.8) | data formatting | bytes 196608
Async XLA Ops:
  0.0 1.1 %copy-start = (bf16[64,768]{1,0:T(8,128)(2,1)S(1)}, bf16[64,768]{1,0:T(8,128)(2,1)}, u32[]{:S(2)}) copy-start(bf16[64,768]{1,0:T(8,128)(2,1)} %refs_0_.1) | copy-start | bytes 294916
  0.0 1.1 %copy-start.1 = (s32[1,32,16]{1,2,0:T(8,128)S(1)}, s32[1,32,16]{1,2,0:T(8,128)}, u32[]{:S(2)}) copy-start(s32[1,32,16]{1,2,0:T(8,128)} %param.6) | copy-start | bytes 6148
  1.1 0.7 %copy-start.2 = (s32[1,32]{1,0:T(1,128)S(1)}, s32[1,32]{1,0:T(1,128)}, u32[]{:S(2)}) copy-start(s32[1,32]{1,0:T(1,128)} %refs_2_.1) | copy-start | bytes 388
  1.1 0.7 %copy-start.3 = (s32[1,64]{1,0:T(1,128)S(1)}, s32[1,64]{1,0:T(1,128)}, u32[]{:S(2)}) copy-start(s32[1,64]{1,0:T(1,128)} %refs_3_.1) | copy-start | bytes 772
